TPU v7x, 32 devices: a whole 2x2x4 slice. The times are simulated.
32 devices in a mesh: seq: 4 (over z), fsdp: 8 (over y, x, core).
Axes of the slice: x: 2, y: 2, z: 4, core: 2. Of those that a mesh axis runs over, the one named last changes fastest.
Arguments:
- inputs: bfloat16 [8, 1024, 2048], P('fsdp', 'seq'), may hold values from -6 to 6
- norm1_gain: bfloat16 [2048], P(('seq', 'fsdp')), may hold values from 0.5 to 1.5
- w_query: bfloat16 [2048, 2048], P(('seq', 'fsdp')), may hold values from -0.125 to 0.125
- w_key: bfloat16 [2048, 2048], P(('seq', 'fsdp')), may hold values from -0.125 to 0.125
- w_value: bfloat16 [2048, 2048], P(('seq', 'fsdp')), may hold values from -0.125 to 0.125
- w_output: bfloat16 [2048, 2048], P(('seq', 'fsdp')), may hold values from -0.5 to 0.5
- norm2_gain: bfloat16 [2048], P(('seq', 'fsdp')), may hold values from 0.5 to 1.5
- w_gate: bfloat16 [2048, 8192], P(('seq', 'fsdp')), may hold values from -0.125 to 0.125
- w_up: bfloat16 [2048, 8192], P(('seq', 'fsdp')), may hold values from -0.125 to 0.125
- w_down: bfloat16 [8192, 2048], P(('seq', 'fsdp')), may hold values from -0.0625 to 0.0625
- out_grad: bfloat16 [8, 1024, 2048], P('fsdp', 'seq'), may hold values from -6 to 6
Outputs:
- output: bfloat16 [8, 1024, 2048], P('fsdp', 'seq')
- input_grad: float32 [8, 1024, 2048], P('fsdp', 'seq')
- norm1_gain_grad: float32 [2048], P(('seq', 'fsdp'))
- w_query_grad: float32 [2048, 2048], P(('seq', 'fsdp'))
- w_key_grad: float32 [2048, 2048], P(('seq', 'fsdp'))
- w_value_grad: float32 [2048, 2048], P(('seq', 'fsdp'))
- w_output_grad: float32 [2048, 2048], P(('seq', 'fsdp'))
- norm2_gain_grad: float32 [2048], P(('seq', 'fsdp'))
- w_gate_grad: float32 [2048, 8192], P(('seq', 'fsdp'))
- w_up_grad: float32 [2048, 8192], P(('seq', 'fsdp'))
- w_down_grad: float32 [8192, 2048], P(('seq', 'fsdp'))
All inputs are finite; a program needn't handle non-finite values.
Results may differ from a plain program's by a relative error of at most 0.014.
Values may be sent and summed in bfloat16 or wider, within the bound.
No kernel may reach another device: no remote copies, remote signals or barrier semaphores. Data moves between devices by JAX's collectives and lax.ppermute only.
A program may use at most 576 MiB of HBM per device.

v0:
```python
import math
import jax
import jax.numpy as jnp
from jax import lax
from jax.sharding import PartitionSpec as P

HEAD_DIM = 64
QBLK = 512
EPS = 1e-05
ROPE_BASE = 130000.0
NEG_FILL = -1e30


def tables(positions):
    half_dim = HEAD_DIM // 2
    freqs = jnp.exp(
        jnp.arange(half_dim, dtype=jnp.float32) * (-2.0 * math.log(ROPE_BASE) / HEAD_DIM)
    )
    angle = positions.astype(jnp.float32)[:, None] * freqs[None, :]
    angle = jnp.concatenate([angle, angle], axis=1)
    return (jnp.cos(angle), jnp.sin(angle))


def rotate_half(values):
    half_dim = values.shape[-1] // 2
    return jnp.concatenate([-values[..., half_dim:], values[..., :half_dim]], axis=-1)


def rotary(values, cosine, sine):
    seq_count, local_len, model_width = values.shape
    shaped = values.reshape(seq_count, local_len, model_width // HEAD_DIM, HEAD_DIM)
    turned = shaped * cosine[None, :, None, :] + rotate_half(shaped) * sine[None, :, None, :]
    return turned.reshape(seq_count, local_len, model_width)


def rotary_back(grads, cosine, sine):
    seq_count, local_len, model_width = grads.shape
    shaped = grads.reshape(seq_count, local_len, model_width // HEAD_DIM, HEAD_DIM)
    turned = shaped * cosine[None, :, None, :] - rotate_half(shaped * sine[None, :, None, :])
    return turned.reshape(seq_count, local_len, model_width)


def matmul(left, right):
    return jnp.dot(left, right, preferred_element_type=jnp.float32)


def outer_sum(left, right):
    return lax.dot_general(
        left, right, (((0,), (0,)), ((), ())), preferred_element_type=jnp.float32
    )


def times_transposed(left, right):
    return lax.dot_general(
        left, right, (((1,), (1,)), ((), ())), preferred_element_type=jnp.float32
    )


def normalize(values, gain):
    inverse = lax.rsqrt(jnp.mean(values * values, axis=1, keepdims=True) + EPS)
    return ((values * inverse * gain).astype(jnp.bfloat16), inverse)


def norm_back(grad_normed, values, inverse, gain):
    scaled = grad_normed * gain
    gain_term = jnp.sum(grad_normed * values * inverse, axis=0)
    value_grad = inverse * (
        scaled - values * inverse * inverse * jnp.mean(scaled * values, axis=1, keepdims=True)
    )
    return (gain_term, value_grad)


def causal_block(query_block, key_heads, block_start):
    score_scale = HEAD_DIM ** (-0.5)
    scores = (
        jnp.einsum("sqhd,skhd->shqk", query_block, key_heads, preferred_element_type=jnp.float32)
        * score_scale
    )
    query_pos = block_start + jnp.arange(query_block.shape[1])
    allowed = jnp.arange(key_heads.shape[1])[None, :] <= query_pos[:, None]
    return jnp.where(allowed, scores, NEG_FILL)


def local(
    inputs,
    norm1_gain,
    w_query,
    w_key,
    w_value,
    w_output,
    norm2_gain,
    w_gate,
    w_up,
    w_down,
    out_grad,
):
    seq_count, local_len, model_width = inputs.shape
    row_count = seq_count * local_len
    score_scale = HEAD_DIM ** (-0.5)
    residual_in = inputs.reshape(row_count, model_width).astype(jnp.float32)
    attn_set = (
        lax.all_gather(norm1_gain, ("seq", "fsdp"), axis=0, tiled=True),
        lax.all_gather(w_query, ("seq", "fsdp"), axis=0, tiled=True),
        lax.all_gather(w_key, ("seq", "fsdp"), axis=0, tiled=True),
        lax.all_gather(w_value, ("seq", "fsdp"), axis=0, tiled=True),
        lax.all_gather(w_output, ("seq", "fsdp"), axis=0, tiled=True),
    )
    gain_one, query_w, key_w, value_w, output_w = attn_set
    normed_one, inverse_one = normalize(residual_in, gain_one.astype(jnp.float32))
    positions = lax.axis_index("seq") * local_len + jnp.arange(local_len, dtype=jnp.int32)
    cosine, sine = tables(positions)
    query_rot = rotary(
        matmul(normed_one, query_w).reshape(seq_count, local_len, model_width), cosine, sine
    ).astype(jnp.bfloat16)
    key_rot = rotary(
        matmul(normed_one, key_w).reshape(seq_count, local_len, model_width), cosine, sine
    ).astype(jnp.bfloat16)
    value_tok = (
        matmul(normed_one, value_w).astype(jnp.bfloat16).reshape(seq_count, local_len, model_width)
    )
    query_h, key_h, value_h = (
        lax.all_to_all(query_rot, "seq", split_axis=2, concat_axis=1, tiled=True),
        lax.all_to_all(key_rot, "seq", split_axis=2, concat_axis=1, tiled=True),
        lax.all_to_all(value_tok, "seq", split_axis=2, concat_axis=1, tiled=True),
    )
    full_len = query_h.shape[1]
    head_width = query_h.shape[2]
    heads_here = head_width // HEAD_DIM
    query_heads = query_h.reshape(seq_count, full_len, heads_here, HEAD_DIM)
    key_heads = key_h.reshape(seq_count, full_len, heads_here, HEAD_DIM)
    value_heads = value_h.reshape(seq_count, full_len, heads_here, HEAD_DIM)
    block_outs = []
    block_lse = []
    for block_start in range(0, full_len, QBLK):
        block_end = block_start + QBLK
        query_block = query_heads[:, block_start:block_end]
        scores = causal_block(query_block, key_heads[:, :block_end], block_start)
        row_max = jnp.max(scores, axis=-1, keepdims=True)
        shifted = jnp.exp(scores - row_max)
        row_sum = jnp.sum(shifted, axis=-1, keepdims=True)
        attn_prob = (shifted / row_sum).astype(jnp.bfloat16)
        block_outs.append(
            jnp.einsum(
                "shqk,skhd->sqhd",
                attn_prob,
                value_heads[:, :block_end],
                preferred_element_type=jnp.float32,
            )
        )
        block_lse.append(row_max + jnp.log(row_sum))
    attended = (
        jnp.concatenate(block_outs, axis=1)
        .astype(jnp.bfloat16)
        .reshape(seq_count, full_len, head_width)
    )
    attended_tok = lax.all_to_all(attended, "seq", split_axis=1, concat_axis=2, tiled=True).reshape(
        row_count, model_width
    )
    mid_stream = residual_in + matmul(attended_tok, output_w)
    gain_two, gate_w, up_w, down_w = (
        lax.all_gather(norm2_gain, ("seq", "fsdp"), axis=0, tiled=True),
        lax.all_gather(w_gate, ("seq", "fsdp"), axis=0, tiled=True),
        lax.all_gather(w_up, ("seq", "fsdp"), axis=0, tiled=True),
        lax.all_gather(w_down, ("seq", "fsdp"), axis=0, tiled=True),
    )
    normed_two, inverse_two = normalize(mid_stream, gain_two.astype(jnp.float32))
    gate_pre = matmul(normed_two, gate_w)
    up_pre = matmul(normed_two, up_w)
    gate_sig = jax.nn.sigmoid(gate_pre)
    hidden = (gate_pre * gate_sig * up_pre).astype(jnp.bfloat16)
    output = (
        (mid_stream + matmul(hidden, down_w))
        .astype(jnp.bfloat16)
        .reshape(seq_count, local_len, model_width)
    )
    grad_out = out_grad.reshape(row_count, model_width).astype(jnp.float32)
    grad_outb = grad_out.astype(jnp.bfloat16)
    down_grad = lax.psum_scatter(
        outer_sum(hidden, grad_outb), ("seq", "fsdp"), scatter_dimension=0, tiled=True
    )
    gain_two, gate_w, up_w, down_w = (
        lax.all_gather(norm2_gain, ("seq", "fsdp"), axis=0, tiled=True),
        lax.all_gather(w_gate, ("seq", "fsdp"), axis=0, tiled=True),
        lax.all_gather(w_up, ("seq", "fsdp"), axis=0, tiled=True),
        lax.all_gather(w_down, ("seq", "fsdp"), axis=0, tiled=True),
    )
    grad_hidden = times_transposed(grad_outb, down_w)
    grad_gate = (grad_hidden * up_pre * gate_sig * (1.0 + gate_pre * (1.0 - gate_sig))).astype(
        jnp.bfloat16
    )
    grad_up = (grad_hidden * gate_pre * gate_sig).astype(jnp.bfloat16)
    grad_normed_two = times_transposed(grad_gate, gate_w) + times_transposed(grad_up, up_w)
    gain_two_term, grad_mid = norm_back(
        grad_normed_two, mid_stream, inverse_two, gain_two.astype(jnp.float32)
    )
    grad_mid = grad_out + grad_mid
    gate_grad, gain_two_grad = (
        lax.psum_scatter(
            outer_sum(normed_two, grad_gate), ("seq", "fsdp"), scatter_dimension=0, tiled=True
        ),
        lax.psum_scatter(gain_two_term, ("seq", "fsdp"), scatter_dimension=0, tiled=True),
    )
    up_grad = lax.psum_scatter(
        outer_sum(normed_two, grad_up), ("seq", "fsdp"), scatter_dimension=0, tiled=True
    )
    gain_one, query_w, key_w, value_w, output_w = (
        lax.all_gather(norm1_gain, ("seq", "fsdp"), axis=0, tiled=True),
        lax.all_gather(w_query, ("seq", "fsdp"), axis=0, tiled=True),
        lax.all_gather(w_key, ("seq", "fsdp"), axis=0, tiled=True),
        lax.all_gather(w_value, ("seq", "fsdp"), axis=0, tiled=True),
        lax.all_gather(w_output, ("seq", "fsdp"), axis=0, tiled=True),
    )
    grad_proj = grad_mid.astype(jnp.bfloat16)
    output_term = outer_sum(attended_tok, grad_proj)
    grad_att = (
        times_transposed(grad_proj, output_w)
        .astype(jnp.bfloat16)
        .reshape(seq_count, local_len, model_width)
    )
    grad_att_h = lax.all_to_all(grad_att, "seq", split_axis=2, concat_axis=1, tiled=True)
    grad_heads = grad_att_h.reshape(seq_count, full_len, heads_here, HEAD_DIM)
    grad_key_sum = jnp.zeros(key_heads.shape, jnp.float32)
    grad_value_sum = jnp.zeros(value_heads.shape, jnp.float32)
    query_parts = []
    for block_index, block_start in enumerate(range(0, full_len, QBLK)):
        block_end = block_start + QBLK
        query_block = query_heads[:, block_start:block_end]
        grad_block = grad_heads[:, block_start:block_end]
        key_part = key_heads[:, :block_end]
        value_part = value_heads[:, :block_end]
        scores = causal_block(query_block, key_part, block_start)
        attn_prob = jnp.exp(scores - block_lse[block_index])
        grad_prob = jnp.einsum(
            "sqhd,skhd->shqk", grad_block, value_part, preferred_element_type=jnp.float32
        )
        row_dot = jnp.sum(attn_prob * grad_prob, axis=-1, keepdims=True)
        grad_score = (attn_prob * (grad_prob - row_dot)).astype(jnp.bfloat16)
        query_parts.append(
            jnp.einsum("shqk,skhd->sqhd", grad_score, key_part, preferred_element_type=jnp.float32)
            * score_scale
        )
        grad_key_sum = grad_key_sum.at[:, :block_end].add(
            jnp.einsum(
                "shqk,sqhd->skhd", grad_score, query_block, preferred_element_type=jnp.float32
            )
            * score_scale
        )
        grad_value_sum = grad_value_sum.at[:, :block_end].add(
            jnp.einsum(
                "shqk,sqhd->skhd",
                attn_prob.astype(jnp.bfloat16),
                grad_block,
                preferred_element_type=jnp.float32,
            )
        )
    grad_query_h = (
        jnp.concatenate(query_parts, axis=1)
        .astype(jnp.bfloat16)
        .reshape(seq_count, full_len, head_width)
    )
    grad_key_h = grad_key_sum.astype(jnp.bfloat16).reshape(seq_count, full_len, head_width)
    grad_value_h = grad_value_sum.astype(jnp.bfloat16).reshape(seq_count, full_len, head_width)
    grad_query_t, grad_key_t, grad_value_t = (
        lax.all_to_all(grad_query_h, "seq", split_axis=1, concat_axis=2, tiled=True),
        lax.all_to_all(grad_key_h, "seq", split_axis=1, concat_axis=2, tiled=True),
        lax.all_to_all(grad_value_h, "seq", split_axis=1, concat_axis=2, tiled=True),
    )
    grad_query = (
        rotary_back(grad_query_t.astype(jnp.float32), cosine, sine)
        .astype(jnp.bfloat16)
        .reshape(row_count, model_width)
    )
    grad_key = (
        rotary_back(grad_key_t.astype(jnp.float32), cosine, sine)
        .astype(jnp.bfloat16)
        .reshape(row_count, model_width)
    )
    grad_value = grad_value_t.reshape(row_count, model_width)
    grad_normed_one = (
        times_transposed(grad_query, query_w)
        + times_transposed(grad_key, key_w)
        + times_transposed(grad_value, value_w)
    )
    gain_one_term, grad_in = norm_back(
        grad_normed_one, residual_in, inverse_one, gain_one.astype(jnp.float32)
    )
    input_grad = (grad_mid + grad_in).reshape(seq_count, local_len, model_width)
    query_grad, key_grad, value_grad, output_grad, gain_one_grad = (
        lax.psum_scatter(
            outer_sum(normed_one, grad_query), ("seq", "fsdp"), scatter_dimension=0, tiled=True
        ),
        lax.psum_scatter(
            outer_sum(normed_one, grad_key), ("seq", "fsdp"), scatter_dimension=0, tiled=True
        ),
        lax.psum_scatter(
            outer_sum(normed_one, grad_value), ("seq", "fsdp"), scatter_dimension=0, tiled=True
        ),
        lax.psum_scatter(output_term, ("seq", "fsdp"), scatter_dimension=0, tiled=True),
        lax.psum_scatter(gain_one_term, ("seq", "fsdp"), scatter_dimension=0, tiled=True),
    )
    return (
        output,
        input_grad,
        gain_one_grad,
        query_grad,
        key_grad,
        value_grad,
        output_grad,
        gain_two_grad,
        gate_grad,
        up_grad,
        down_grad,
    )


def solution(mesh):
    in_specs = (
        P("fsdp", "seq", None),
        P(("seq", "fsdp")),
        P(("seq", "fsdp"), None),
        P(("seq", "fsdp"), None),
        P(("seq", "fsdp"), None),
        P(("seq", "fsdp"), None),
        P(("seq", "fsdp")),
        P(("seq", "fsdp"), None),
        P(("seq", "fsdp"), None),
        P(("seq", "fsdp"), None),
        P("fsdp", "seq", None),
    )
    out_specs = (
        P("fsdp", "seq", None),
        P("fsdp", "seq", None),
        P(("seq", "fsdp")),
        P(("seq", "fsdp"), None),
        P(("seq", "fsdp"), None),
        P(("seq", "fsdp"), None),
        P(("seq", "fsdp"), None),
        P(("seq", "fsdp")),
        P(("seq", "fsdp"), None),
        P(("seq", "fsdp"), None),
        P(("seq", "fsdp"), None),
    )
    return jax.shard_map(local, mesh=mesh, in_specs=in_specs, out_specs=out_specs, check_vma=False)
```

profile of v0, /device:TPU:14, one launch (start us, length us, event | category | flops | bytes accessed | tf_op | source)
XLA Modules:
  0.0 3977.1 jit_solution(12633569938991020945)
XLA Ops:
  12.4 40.6 %all-reduce.7 = (bf16[2048]{0:T(1024)(128)(2,1)S(1)}, bf16[2048]{0:T(1024)(128)(2,1)S(1)}) all-reduce(bf16[2048]{0:T(1024)(128)(2,1)S(1)} %dynamic-update-slice.10, bf16[2048]{0:T(1024)(128)(2,1)S(1)} %dynamic-update-slice.11), channel_id=1, replica_groups=mesh['seq'=4,'fsdp'=8] {'seq','fsdp'}, use_global_device_ids=true, to_apply=%add.2 | all-reduce | flops 4096 | bytes 16384
  60.9 28.0 all-gather.8.cloned.1.call-done
  88.9 5.8 fusion.20
  98.9 11.7 reduce.20
  112.2 4.9 all-to-all-start
  117.1 66.3 %all-gather.12.cloned.1.call-done = bf16[2048,2048]{1,0:T(8,128)(2,1)} async-done(((bf16[64,2048]{1,0:T(8,128)(2,1)}), bf16[2048,2048]{1,0:T(8,128)(2,1)}) %all-gather.12.cloned.1.call-update) | async-done | bytes 8388624 | tf_op jit(solution)/shard_map/all_gather | solution.py:104
  183.4 7.1 fusion.69
  193.4 69.0 %all-gather.10.cloned.1.call-done = bf16[2048,2048]{1,0:T(8,128)(2,1)} async-done(((bf16[64,2048]{1,0:T(8,128)(2,1)}), bf16[2048,2048]{1,0:T(8,128)(2,1)}) %all-gather.10.cloned.1.call-update) | async-done | bytes 8388624 | tf_op jit(solution)/shard_map/all_gather | solution.py:103
  262.4 7.2 fusion.71
  283.3 6.2 fusion.49
  293.3 11.6 reduce.21
  314.3 11.6 reduce.22
  327.6 28.2 all-to-all-done.2
  355.8 8.1 all-to-all-start.1
  382.0 20.6 all-to-all-done.1
  424.9 4.3 fusion.74
  435.2 4.5 fusion.48
  446.3 8.0 reduce.23
  456.3 6.8 all-to-all-start.3
  463.2 44.9 %all-to-all-done.3 = bf16[4,2,65536]{2,1,0:T(2,128)(2,1)S(1)} async-done(((bf16[4,2,65536]{2,1,0:T(2,128)(2,1)}), bf16[4,2,65536]{2,1,0:T(2,128)(2,1)S(1)}, u32[]{:S(2)}, u32[]{:S(2)}) %all-to-all-start.3) | async-done | bytes 1048608 | tf_op jit(solution)/shard_map/all_to_all | solution.py:156
  513.1 5.8 multiply_reduce_fusion.4
  520.5 56.0 %all-gather.18.cloned.1.call-done = bf16[2048,8192]{1,0:T(8,128)(2,1)} async-done(((bf16[64,8192]{1,0:T(8,128)(2,1)}), bf16[2048,8192]{1,0:T(8,128)(2,1)}) %all-gather.18.cloned.1.call-update) | async-done | bytes 33554448 | tf_op jit(solution)/shard_map/all_gather | solution.py:163
  576.6 17.1 fusion.79
  593.7 183.1 %all-gather.16.cloned.1.call-done = bf16[2048,8192]{1,0:T(8,128)(2,1)} async-done(((bf16[64,8192]{1,0:T(8,128)(2,1)}), bf16[2048,8192]{1,0:T(8,128)(2,1)}) %all-gather.16.cloned.1.call-update) | async-done | bytes 33554448 | tf_op jit(solution)/shard_map/all_gather | solution.py:162
  776.8 17.1 fusion.78
  793.9 178.7 %all-gather.20.cloned.1.call-done = bf16[8192,2048]{1,0:T(8,128)(2,1)} async-done(((bf16[256,2048]{1,0:T(8,128)(2,1)}), bf16[8192,2048]{1,0:T(8,128)(2,1)}) %all-gather.20.cloned.1.call-update) | async-done | bytes 33554448 | tf_op jit(solution)/shard_map/all_gather | solution.py:164
  972.6 24.4 multiply_convert_fusion.2
  997.1 17.0 fusion.80
  1014.1 16.9 multiply_reduce_fusion.2
  1033.0 8.1 fusion.56
  1041.1 6.4 fusion.21
  1051.3 11.6 reduce.24
  1064.6 5.9 all-to-all-start.4
  1070.5 28.8 all-to-all-done.4
  1105.3 4.8 fusion.41
  1110.1 7.6 fusion.35
  1121.6 8.0 reduce.27
  1131.6 58.2 %all_to_all.108 = bf16[4,2,65536]{2,1,0:T(2,128)(2,1)S(1)} all-to-all(bf16[4,2,65536]{2,1,0:T(2,128)(2,1)} %reshape.887), channel_id=1, replica_groups=mesh['seq'=4,'fsdp'=8] {'seq'}, dimensions={0} | all-to-all | bytes 2097152 | tf_op jit(solution)/shard_map/all_to_all | solution.py:266
  1196.5 8.3 fusion.63
  1206.0 4.5 multiply_reduce_fusion.1
  1210.6 4.6 multiply_convert_fusion.1
  1220.1 8.3 multiply_reduce_fusion
  1228.4 7.9 multiply_convert_fusion
  1246.8 8.0 reduce.26
  1256.8 8.9 all-to-all-start.5
  1269.4 5.1 fusion.36
  1278.3 8.0 reduce.25
  1288.4 5.3 all-to-all-done.5
  1293.7 11.5 all-to-all-start.6
  1305.2 4.3 reshape.884
  1316.0 17.4 all-to-all-done.6
  1350.2 8.3 fusion.67
  1358.6 8.3 fusion.65
  1368.1 26.2 fusion.52
  1395.5 26.3 fusion.83
  1421.9 26.2 fusion.82
  1449.7 17.6 fusion.22
  1470.1 7.3 fusion.81
  1486.0 53.6 %all-reduce.6 = (f32[2048]{0:T(1024)S(1)}, f32[2048]{0:T(1024)S(1)}) all-reduce(f32[2048]{0:T(1024)S(1)} %get-tuple-element.77, f32[2048]{0:T(1024)S(1)} %copy-done.48), channel_id=2, replica_groups=mesh['seq'=4,'fsdp'=8] {'seq','fsdp'}, use_global_device_ids=true, to_apply=%region_11.12.clone | all-reduce | flops 4096 | bytes 32768
  1544.4 100.8 %reduce-scatter.8.cloned.1.call-done = f32[64,2048]{1,0:T(8,128)} async-done(((f32[2048,2048]{1,0:T(8,128)}), f32[64,2048]{1,0:T(8,128)}) %reduce-scatter.8.cloned.1.call-update) | async-done | bytes 524304 | tf_op jit(solution)/shard_map/reduce_scatter | solution.py:289
  1645.1 187.4 %reduce-scatter.10.cloned.1.call-done = f32[64,2048]{1,0:T(8,128)} async-done(((f32[2048,2048]{1,0:T(8,128)}), f32[64,2048]{1,0:T(8,128)}) %reduce-scatter.10.cloned.1.call-update) | async-done | bytes 524304 | tf_op jit(solution)/shard_map/reduce_scatter | solution.py:292
  1832.5 711.7 %reduce-scatter.20.cloned.1.call-done = f32[256,2048]{1,0:T(8,128)} async-done(((f32[8192,2048]{1,0:T(8,128)}), f32[256,2048]{1,0:T(8,128)}) %reduce-scatter.20.cloned.1.call-update) | async-done | bytes 2097168 | tf_op jit(solution)/shard_map/reduce_scatter | solution.py:178
  2544.2 713.2 %reduce-scatter.18.cloned.1.call-done = f32[64,8192]{1,0:T(8,128)} async-done(((f32[2048,8192]{1,0:T(8,128)}), f32[64,8192]{1,0:T(8,128)}) %reduce-scatter.18.cloned.1.call-update) | async-done | bytes 2097168 | tf_op jit(solution)/shard_map/reduce_scatter | solution.py:203
  3257.4 713.0 %reduce-scatter.16.cloned.1.call-done = f32[64,8192]{1,0:T(8,128)} async-done(((f32[2048,8192]{1,0:T(8,128)}), f32[64,8192]{1,0:T(8,128)}) %reduce-scatter.16.cloned.1.call-update) | async-done | bytes 2097168 | tf_op jit(solution)/shard_map/reduce_scatter | solution.py:198
  (247 shorter events, 208.7 us)
Async XLA Ops:
  7.2 4.7 copy-start.49
  7.2 5.0 copy-start.50
  7.2 81.7 %all-gather.8.cloned.1.call-start = ((), (), s32[]{:S(2)}) async-start(), calls=%async_computation.15 | async-start | bytes 8650752 | tf_op jit(solution)/shard_map/all_gather | solution.py:105
  7.9 175.5 %all-gather.12.cloned.1.call-start = ((), (), s32[]{:S(2)}) async-start(), calls=%async_computation.17 | async-start | bytes 8650752 | tf_op jit(solution)/shard_map/all_gather | solution.py:104
  8.7 253.7 %all-gather.10.cloned.1.call-start = ((), (), s32[]{:S(2)}) async-start(), calls=%async_computation.16 | async-start | bytes 8650752 | tf_op jit(solution)/shard_map/all_gather | solution.py:103
  9.4 503.7 %all-gather.14.cloned.1.call-start = ((), (), s32[]{:S(2)}) async-start(), calls=%async_computation.18 | async-start | bytes 8650752 | tf_op jit(solution)/shard_map/all_gather | solution.py:106
  10.0 566.6 %all-gather.18.cloned.1.call-start = ((), (), s32[]{:S(2)}) async-start(), calls=%async_computation.20 | async-start | bytes 34603008 | tf_op jit(solution)/shard_map/all_gather | solution.py:163
  10.6 766.2 %all-gather.16.cloned.1.call-start = ((), (), s32[]{:S(2)}) async-start(), calls=%async_computation.19 | async-start | bytes 34603008 | tf_op jit(solution)/shard_map/all_gather | solution.py:162
  11.2 961.5 %all-gather.20.cloned.1.call-start = ((), (), s32[]{:S(2)}) async-start(), calls=%async_computation.21 | async-start | bytes 34603008 | tf_op jit(solution)/shard_map/all_gather | solution.py:164
  53.0 209.3 %copy-start.38 = (f32[2048]{0:T(1024)}, f32[2048]{0:T(1024)S(1)}, u32[]{:S(2)}) copy-start(f32[2048]{0:T(1024)S(1)} %convert_element_type.262) | copy-start | bytes 24580
  53.3 2.7 copy-start.33
  57.5 3.0 copy-start.3
  60.8 201.5 %copy-start.43 = (f32[256]{0:T(256)}, f32[256]{0:T(256)S(1)}, u32[]{:S(2)}) copy-start(f32[256]{0:T(256)S(1)} %add_rsqrt_fusion.1) | copy-start | bytes 3076
  112.2 194.4 %all-to-all-start = ((bf16[4,2,65536]{2,1,0:T(2,128)(2,1)}), bf16[4,2,65536]{2,1,0:T(2,128)(2,1)}, u32[]{:S(2)}, u32[]{:S(2)}) async-start(bf16[4,2,65536]{2,1,0:T(2,128)(2,1)} %reshape.873), calls=%async_computation | async-start | bytes 2097152 | tf_op jit(solution)/shard_map/all_to_all | solution.py:124
  262.4 7.2 copy-start.22
  306.6 49.2 %all-to-all-start.2 = ((bf16[4,2,65536]{2,1,0:T(2,128)(2,1)}), bf16[4,2,65536]{2,1,0:T(2,128)(2,1)S(1)}, u32[]{:S(2)}, u32[]{:S(2)}) async-start(bf16[4,2,65536]{2,1,0:T(2,128)(2,1)} %reshape.875), calls=%async_computation.2 | async-start | bytes 2097152 | tf_op jit(solution)/shard_map/all_to_all | solution.py:123
  355.8 46.7 %all-to-all-start.1 = ((bf16[4,2,65536]{2,1,0:T(2,128)(2,1)}), bf16[4,2,65536]{2,1,0:T(2,128)(2,1)}, u32[]{:S(2)}, u32[]{:S(2)}) async-start(bf16[4,2,65536]{2,1,0:T(2,128)(2,1)} %reshape.877), calls=%async_computation.1 | async-start | bytes 2097152 | tf_op jit(solution)/shard_map/all_to_all | solution.py:122
  380.4 44.5 %copy-start.19 = (bf16[1024,8,64]{0,2,1:T(8,128)(2,1)}, bf16[1024,8,64]{0,2,1:T(8,128)(2,1)S(1)}, u32[]{:S(2)}) copy-start(bf16[1024,8,64]{0,2,1:T(8,128)(2,1)S(1)} %reshape.847) | copy-start | bytes 3145732
  411.8 13.1 copy-start.15
  414.8 4.1 copy-start.1
  414.8 4.1 copy-start.41
  414.8 4.1 copy-start.31
  429.2 6.0 copy-start
  429.2 6.0 copy-start.27
  439.6 2.5 copy-start.30
  456.3 51.8 %all-to-all-start.3 = ((bf16[4,2,65536]{2,1,0:T(2,128)(2,1)}), bf16[4,2,65536]{2,1,0:T(2,128)(2,1)S(1)}, u32[]{:S(2)}, u32[]{:S(2)}) async-start(bf16[4,2,65536]{2,1,0:T(2,128)(2,1)} %reshape.879), calls=%async_computation.3 | async-start | bytes 2097152 | tf_op jit(solution)/shard_map/all_to_all | solution.py:156
  463.2 1081.2 %reduce-scatter.14.cloned.1.call-start = ((), (), s32[]{:S(2)}) async-start(), calls=%async_computation.25 | async-start | bytes 17301504 | tf_op jit(solution)/shard_map/reduce_scatter | solution.py:298
  520.5 256.3 %copy-start.17 = (bf16[256,2048]{1,0:T(8,128)(2,1)}, bf16[256,2048]{1,0:T(8,128)(2,1)S(1)}, u32[]{:S(2)}) copy-start(bf16[256,2048]{1,0:T(8,128)(2,1)S(1)} %multiply_convert_fusion.5) | copy-start | bytes 3145732
  997.1 17.0 copy-start.13
  1014.1 16.9 copy-start.23
  1062.9 7.6 copy-start.42
  1062.9 7.6 copy-start.47
  1064.6 34.8 all-to-all-start.4
  1070.5 473.8 %reduce-scatter.12.cloned.1.call-start = ((), (), s32[]{:S(2)}) async-start(), calls=%async_computation.24 | async-start | bytes 17301504 | tf_op jit(solution)/shard_map/reduce_scatter | solution.py:295
  1192.1 4.4 copy-start.39
  1192.1 4.4 copy-start.44
  1196.5 8.3 copy-start.25
  1210.6 6.7 copy-start.28
  1228.4 7.9 copy-start.20
  1236.4 3.6 copy-start.2
  1239.9 2.7 copy-start.29
  1254.8 10.9 copy-start.16
  1256.8 36.9 all-to-all-start.5
  1293.7 39.7 all-to-all-start.6
  1305.2 339.9 %reduce-scatter.8.cloned.1.call-start = ((), (), s32[]{:S(2)}) async-start(), calls=%async_computation.22 | async-start | bytes 17301504 | tf_op jit(solution)/shard_map/reduce_scatter | solution.py:289
  1339.2 3.0 copy-start.37
  1358.5 474.0 %reduce-scatter.10.cloned.1.call-start = ((), (), s32[]{:S(2)}) async-start(), calls=%async_computation.23 | async-start | bytes 17301504 | tf_op jit(solution)/shard_map/reduce_scatter | solution.py:292
  1366.9 1177.3 %reduce-scatter.20.cloned.1.call-start = ((), (), s32[]{:S(2)}) async-start(), calls=%async_computation.28 | async-start | bytes 69206016 | tf_op jit(solution)/shard_map/reduce_scatter | solution.py:178
  1394.3 1863.1 %reduce-scatter.18.cloned.1.call-start = ((), (), s32[]{:S(2)}) async-start(), calls=%async_computation.27 | async-start | bytes 69206016 | tf_op jit(solution)/shard_map/reduce_scatter | solution.py:203
  1421.8 2548.5 %reduce-scatter.16.cloned.1.call-start = ((), (), s32[]{:S(2)}) async-start(), calls=%async_computation.26 | async-start | bytes 69206016 | tf_op jit(solution)/shard_map/reduce_scatter | solution.py:198
  1449.7 17.7 copy-start.7
  1449.7 17.7 copy-start.9
  1449.7 17.7 copy-start.21
  1449.7 17.7 copy-start.35
  1467.4 10.0 slice-start.2
  1470.1 7.4 slice-start.3
  1470.1 11.6 slice-start
  1477.4 4.3 copy-start.4
  1477.4 4.3 copy-start.26
  1477.4 4.3 copy-start.40
  1477.4 4.3 copy-start.45
  1477.4 4.3 slice-start.1
  1481.8 4.2 copy-start.48
  1481.8 59.0 %copy-start.11 = (f32[256,2048]{1,0:T(8,128)S(1)}, f32[256,2048]{1,0:T(8,128)}, u32[]{:S(2)}) copy-start(f32[256,2048]{1,0:T(8,128)} %copy-done.10) | copy-start | bytes 6291460
  (12 other events, 19.0 us)
Sparse Core Ops, SparseCore 0:
  10.9 77.9 all-gather.7
  91.7 91.6 all-gather.11
  186.3 76.0 all-gather.9
  265.1 91.3 all-gather.13
  359.2 217.3 all-gather.17
  579.3 197.4 all-gather.15
  779.7 192.9 all-gather.19
  1041.3 203.7 reduce-scatter.13
  1247.9 209.0 reduce-scatter.11
  1459.7 185.4 reduce-scatter.7
  1648.0 184.4 reduce-scatter.9
  1835.3 708.8 reduce-scatter.19
  2547.1 710.2 reduce-scatter.17
  3260.2 710.1 reduce-scatter.15
where the time goes:
time: 3990 us; the launch traced here: 3980 us
  waiting for transfers between devices  3160 us (79%)
  matrix products  322 us (8%)
  blocking collectives  152 us (4%)
  local copies, waits for them, and re-layouts  146 us (4%)
  other arithmetic  134 us (3%)
  starting transfers between devices  50.6 us (1%)
    reduce_scatter x1, waiting for transfers between devices, local(): lax.psum_scatter(outer_sum(normed_two, grad_up), ('seq', 'fsdp'), scatter...  713 us
    reduce_scatter x1, waiting for transfers between devices, local(): lax.psum_scatter(outer_sum(normed_two, grad_gate), ('seq', 'fsdp'), scatt...  713 us
    reduce_scatter x1, waiting for transfers between devices, local(): lax.psum_scatter(outer_sum(hidden, grad_outb), ('seq', 'fsdp'), scatter_d...  712 us
    reduce_scatter x1, waiting for transfers between devices, local(): lax.psum_scatter(outer_sum(normed_one, grad_key), ('seq', 'fsdp'), scatte...  187 us
    all_gather x1, waiting for transfers between devices, local(): lax.all_gather(w_gate, ('seq', 'fsdp'), axis=0, tiled=True)  183 us
    all_gather x1, waiting for transfers between devices, local(): lax.all_gather(w_down, ('seq', 'fsdp'), axis=0, tiled=True)  179 us
    dot_general x7, matrix products, outer_sum(): lax.dot_general(left, right, (((0,), (0,)), ((), ())), preferred_element_...  112 us
    reduce_scatter x1, waiting for transfers between devices, local(): lax.psum_scatter(outer_sum(normed_one, grad_query), ('seq', 'fsdp'), scat...  101 us
  transfers between devices with their start and end apart: 21, of which 17 were waited for; matrix products, arithmetic and copies ran while one was open for 13% of the time, Pallas kernels for 0%

commit v1 on v0

--- a/solution.py
+++ b/solution.py
@@ -9,6 +9,21 @@
 EPS = 1e-05
 ROPE_BASE = 130000.0
 NEG_FILL = -1e30
+
+
+def wall_view(block_here, net_axis, out_dim):
+    v1, later = (jax.lax.axis_size(net_axis), jax.lax.axis_index(net_axis))
+    z2, value_now = (block_here, 1)
+    while value_now < v1:
+        line_up = []
+        for nth in range(v1):
+            line_up.append((nth, nth ^ value_now))
+        frame_out = jax.lax.ppermute(z2, net_axis, line_up)
+        state_now = jnp.concatenate([z2, frame_out], axis=out_dim)
+        res = jnp.concatenate([frame_out, z2], axis=out_dim)
+        z2 = jnp.where(later & value_now == 0, state_now, res)
+        value_now = 2 * value_now
+    return z2
 
 
 def tables(positions):
@@ -159,7 +174,7 @@
     mid_stream = residual_in + matmul(attended_tok, output_w)
     gain_two, gate_w, up_w, down_w = (
         lax.all_gather(norm2_gain, ("seq", "fsdp"), axis=0, tiled=True),
-        lax.all_gather(w_gate, ("seq", "fsdp"), axis=0, tiled=True),
+        wall_view(w_gate, ("seq", "fsdp"), 0),
         lax.all_gather(w_up, ("seq", "fsdp"), axis=0, tiled=True),
         lax.all_gather(w_down, ("seq", "fsdp"), axis=0, tiled=True),
     )

time: 3990 us -> 4900 us (1.23)
  waiting for transfers between devices: 3160 us -> 3740 us
  blocking collectives: 152 us -> 400 us
    all_to_all x1, waiting for transfers between devices: 20.6 us -> 683 us  [local(): lax.all_to_all(query_rot, 'seq', split_axis=2, concat_axis=1, tiled=True)]
    all_to_all x1, waiting for transfers between devices: 28.2 us -> 364 us  [local(): lax.all_to_all(key_rot, 'seq', split_axis=2, concat_axis=1, tiled=True)]
    unnamed x2, blocking collectives: 94.2 us -> 353 us
    reduce_scatter x1, waiting for transfers between devices: 0.01 us -> 187 us  [local(): lax.psum_scatter(outer_sum(normed_one, grad_value), ('seq', 'fsdp'), scat...]
    all_gather x1, waiting for transfers between devices: 183 us -> 0.01 us  [local(): lax.all_gather(w_gate, ('seq', 'fsdp'), axis=0, tiled=True)]
    all_gather x1, waiting for transfers between devices: 179 us -> 0.02 us  [local(): lax.all_gather(w_down, ('seq', 'fsdp'), axis=0, tiled=True)]
    ppermute x0 -> x5, waiting for transfers between devices: none -> 176 us  [wall_view(): frame_out = jax.lax.ppermute(z2, net_axis, line_up)]
    reduce_scatter x1, waiting for transfers between devices: 101 us -> 0.01 us  [local(): lax.psum_scatter(outer_sum(normed_one, grad_query), ('seq', 'fsdp'), scat...]
  transfers between devices with their start and end apart: 21 -> 26, of which waited for: 17 -> 13; matrix products, arithmetic and copies ran while one was open for 13% -> 12% of each run, Pallas kernels for 0% -> 0%
where the time goes in v1:
time: 4900 us; the launch traced here: 4890 us
  waiting for transfers between devices  3740 us (76%)
  blocking collectives  400 us (8%)
  matrix products  339 us (7%)
  other arithmetic  176 us (4%)
  local copies, waits for them, and re-layouts  152 us (3%)
  starting transfers between devices  67.3 us (1%)
    reduce_scatter x1, waiting for transfers between devices, local(): lax.psum_scatter(outer_sum(normed_two, grad_up), ('seq', 'fsdp'), scatter...  713 us
    reduce_scatter x1, waiting for transfers between devices, local(): lax.psum_scatter(outer_sum(hidden, grad_outb), ('seq', 'fsdp'), scatter_d...  713 us
    reduce_scatter x1, waiting for transfers between devices, local(): lax.psum_scatter(outer_sum(normed_two, grad_gate), ('seq', 'fsdp'), scatt...  712 us
    all_to_all x1, waiting for transfers between devices, local(): lax.all_to_all(query_rot, 'seq', split_axis=2, concat_axis=1, tiled=True)  683 us
    all_to_all x1, waiting for transfers between devices, local(): lax.all_to_all(key_rot, 'seq', split_axis=2, concat_axis=1, tiled=True)  364 us
    unnamed x2, blocking collectives  353 us
    reduce_scatter x1, waiting for transfers between devices, local(): lax.psum_scatter(outer_sum(normed_one, grad_value), ('seq', 'fsdp'), scat...  187 us
    ppermute x5, waiting for transfers between devices, wall_view(): frame_out = jax.lax.ppermute(z2, net_axis, line_up)  176 us
  transfers between devices with their start and end apart: 26, of which 13 were waited for; matrix products, arithmetic and copies ran while one was open for 12% of the time, Pallas kernels for 0%

profile of v1, /device:TPU:14, one launch (start us, length us, event | category | flops | bytes accessed | tf_op | source)
XLA Modules:
  0.0 4889.9 jit_solution(2343078704914833717)
XLA Ops:
  17.4 61.3 %collective-permute-done.1 = bf16[128,8192]{1,0:T(8,128)(2,1)} collective-permute-done((bf16[128,8192]{1,0:T(8,128)(2,1)S(1)}, bf16[128,8192]{1,0:T(8,128)(2,1)}, u32[]{:S(2)}, u32[]{:S(2)}) %collective-permute-start.1) | collective-permute-done | bytes 2097184 | tf_op jit(solution)/shard_map/ppermute | solution.py:21
  83.6 111.8 %collective-permute-done.2 = bf16[256,8192]{1,0:T(8,128)(2,1)} collective-permute-done((bf16[256,8192]{1,0:T(8,128)(2,1)}, bf16[256,8192]{1,0:T(8,128)(2,1)}, u32[]{:S(2)}, u32[]{:S(2)}) %collective-permute-start.2) | collective-permute-done | bytes 4194336 | tf_op jit(solution)/shard_map/ppermute | solution.py:21
  195.4 10.9 maximum_select_fusion.3
  207.1 310.3 %all-reduce.7 = (bf16[2048]{0:T(1024)(128)(2,1)S(1)}, bf16[2048]{0:T(1024)(128)(2,1)S(1)}) all-reduce(bf16[2048]{0:T(1024)(128)(2,1)S(1)} %dynamic-update-slice.10, bf16[2048]{0:T(1024)(128)(2,1)S(1)} %dynamic-update-slice.11), channel_id=1, replica_groups=mesh['seq'=4,'fsdp'=8] {'seq','fsdp'}, use_global_device_ids=true, to_apply=%add.2 | all-reduce | flops 4096 | bytes 16384
  526.0 6.7 fusion.27
  532.7 5.9 copy.121
  539.2 12.6 reduce.20
  555.2 5.7 all-to-all-start
  560.9 7.2 fusion.79
  571.0 7.2 fusion.77
  592.0 6.9 fusion.56
  603.5 11.6 reduce.21
  618.5 5.1 all-to-all-start.2
  623.6 20.5 maximum_select_fusion.2
  646.6 4.6 copy.127
  651.2 11.6 reduce.22
  666.2 364.0 %all-to-all-done.2 = bf16[4,2,65536]{2,1,0:T(2,128)(2,1)} async-done(((bf16[4,2,65536]{2,1,0:T(2,128)(2,1)}), bf16[4,2,65536]{2,1,0:T(2,128)(2,1)}, u32[]{:S(2)}, u32[]{:S(2)}) %all-to-all-start.2) | async-done | bytes 1048608 | tf_op jit(solution)/shard_map/all_to_all | solution.py:138
  1030.3 7.9 all-to-all-start.1
  1055.0 682.8 %all-to-all-done.1 = bf16[4,2,65536]{2,1,0:T(2,128)(2,1)} async-done(((bf16[4,2,65536]{2,1,0:T(2,128)(2,1)}), bf16[4,2,65536]{2,1,0:T(2,128)(2,1)}, u32[]{:S(2)}, u32[]{:S(2)}) %all-to-all-start.1) | async-done | bytes 1048608 | tf_op jit(solution)/shard_map/all_to_all | solution.py:137
  1747.1 4.6 fusion.82
  1778.6 8.0 reduce.23
  1790.4 7.7 all-to-all-start.3
  1798.0 23.0 all-to-all-done.3
  1827.3 6.2 multiply_reduce_fusion.4
  1833.8 19.3 fusion.61
  1853.2 17.0 fusion.86
  1870.2 33.4 multiply_convert_fusion.2
  1903.6 15.4 fusion.87
  1919.0 16.6 multiply_reduce_fusion.2
  1938.0 8.1 fusion.63
  1946.2 5.7 fusion.28
  1953.7 10.7 reduce.24
  1966.0 7.1 all-to-all-start.4
  1973.1 28.2 all-to-all-done.4
  2004.1 7.9 multiply_reduce_fusion.1
  2012.0 7.6 multiply_convert_fusion.1
  2024.1 9.5 multiply_reduce_fusion
  2033.6 7.9 multiply_convert_fusion
  2045.1 5.0 copy.150
  2050.2 8.1 reduce.25
  2062.0 16.2 all-to-all-start.6
  2078.2 7.0 fusion.52
  2098.3 8.0 reduce.26
  2110.1 13.2 all-to-all-start.5
  2128.3 23.0 all-to-all-done.5
  2168.4 8.2 fusion.75
  2177.9 8.4 fusion.73
  2187.5 4.9 fusion.48
  2192.4 8.9 fusion.42
  2201.3 4.6 copy.155
  2205.9 8.0 reduce.27
  2216.5 47.3 all_to_all.108
  2269.2 8.3 fusion.71
  2278.7 26.3 fusion.89
  2305.1 26.2 fusion.90
  2332.6 26.1 fusion.59
  2360.3 17.7 fusion.29
  2380.8 7.4 fusion.88
  2396.7 42.5 all-reduce.6
  2443.9 113.9 %reduce-scatter.10.cloned.1.call-done = f32[64,2048]{1,0:T(8,128)} async-done(((f32[2048,2048]{1,0:T(8,128)}), f32[64,2048]{1,0:T(8,128)}) %reduce-scatter.10.cloned.1.call-update) | async-done | bytes 524304 | tf_op jit(solution)/shard_map/reduce_scatter | solution.py:307
  2557.8 187.4 %reduce-scatter.12.cloned.1.call-done = f32[64,2048]{1,0:T(8,128)} async-done(((f32[2048,2048]{1,0:T(8,128)}), f32[64,2048]{1,0:T(8,128)}) %reduce-scatter.12.cloned.1.call-update) | async-done | bytes 524304 | tf_op jit(solution)/shard_map/reduce_scatter | solution.py:310
  2745.3 711.6 %reduce-scatter.16.cloned.1.call-done = f32[64,8192]{1,0:T(8,128)} async-done(((f32[2048,8192]{1,0:T(8,128)}), f32[64,8192]{1,0:T(8,128)}) %reduce-scatter.16.cloned.1.call-update) | async-done | bytes 2097168 | tf_op jit(solution)/shard_map/reduce_scatter | solution.py:213
  3456.8 713.2 %reduce-scatter.18.cloned.1.call-done = f32[64,8192]{1,0:T(8,128)} async-done(((f32[2048,8192]{1,0:T(8,128)}), f32[64,8192]{1,0:T(8,128)}) %reduce-scatter.18.cloned.1.call-update) | async-done | bytes 2097168 | tf_op jit(solution)/shard_map/reduce_scatter | solution.py:218
  4170.1 713.1 %reduce-scatter.20.cloned.1.call-done = f32[256,2048]{1,0:T(8,128)} async-done(((f32[8192,2048]{1,0:T(8,128)}), f32[256,2048]{1,0:T(8,128)}) %reduce-scatter.20.cloned.1.call-update) | async-done | bytes 2097168 | tf_op jit(solution)/shard_map/reduce_scatter | solution.py:193
  (286 shorter events, 211.4 us)
Async XLA Ops:
  7.2 518.8 %all-gather.8.cloned.1.call-start = ((), (), s32[]{:S(2)}) async-start(), calls=%async_computation.15 | async-start | bytes 8650752 | tf_op jit(solution)/shard_map/all_gather | solution.py:120
  7.9 553.0 %all-gather.10.cloned.1.call-start = ((), (), s32[]{:S(2)}) async-start(), calls=%async_computation.16 | async-start | bytes 8650752 | tf_op jit(solution)/shard_map/all_gather | solution.py:118
  8.7 562.3 %all-gather.12.cloned.1.call-start = ((), (), s32[]{:S(2)}) async-start(), calls=%async_computation.17 | async-start | bytes 8650752 | tf_op jit(solution)/shard_map/all_gather | solution.py:119
  9.4 1817.9 %all-gather.14.cloned.1.call-start = ((), (), s32[]{:S(2)}) async-start(), calls=%async_computation.18 | async-start | bytes 8650752 | tf_op jit(solution)/shard_map/all_gather | solution.py:121
  10.0 1823.8 %all-gather.18.cloned.1.call-start = ((), (), s32[]{:S(2)}) async-start(), calls=%async_computation.20 | async-start | bytes 34603008 | tf_op jit(solution)/shard_map/all_gather | solution.py:179
  10.6 1842.6 %all-gather.16.cloned.1.call-start = ((), (), s32[]{:S(2)}) async-start(), calls=%async_computation.19 | async-start | bytes 34603008 | tf_op jit(solution)/shard_map/all_gather | solution.py:178
  11.1 1892.5 %all-gather.20.cloned.1.call-start = ((), (), s32[]{:S(2)}) async-start(), calls=%async_computation.21 | async-start | bytes 34603008 | tf_op jit(solution)/shard_map/all_gather | solution.py:198
  11.9 2.9 collective-permute-start
  16.8 61.9 %collective-permute-start.1 = (bf16[128,8192]{1,0:T(8,128)(2,1)S(1)}, bf16[128,8192]{1,0:T(8,128)(2,1)}, u32[]{:S(2)}, u32[]{:S(2)}) collective-permute-start(bf16[128,8192]{1,0:T(8,128)(2,1)S(1)} %maximum_select_fusion.5), channel_id=1, source_target_pairs={{0,2},{1,3},{2,0},{3,1},{4,6},{5,7},{6,4},{7,5},{8,10},{9,11},{10,... | collective-permute-start | bytes 6291464 | tf_op jit(solution)/shard_map/ppermute | solution.py:21
  83.1 112.2 %collective-permute-start.2 = (bf16[256,8192]{1,0:T(8,128)(2,1)}, bf16[256,8192]{1,0:T(8,128)(2,1)}, u32[]{:S(2)}, u32[]{:S(2)}) collective-permute-start(bf16[256,8192]{1,0:T(8,128)(2,1)} %maximum_select_fusion.4), channel_id=1, source_target_pairs={{0,4},{1,5},{2,6},{3,7},{4,0},{5,1},{6,2},{7,3},{8,12},{9,13},{10,... | collective-permute-start | bytes 12582920 | tf_op jit(solution)/shard_map/ppermute | solution.py:21
  83.6 123.1 %copy-start.57 = (bf16[64]{0:T(256)(128)(2,1)S(1)}, bf16[64]{0:T(256)(128)(2,1)}, u32[]{:S(2)}) copy-start(bf16[64]{0:T(256)(128)(2,1)} %param.24) | copy-start | bytes 388
  83.6 123.3 %copy-start.58 = (bf16[64]{0:T(256)(128)(2,1)S(1)}, bf16[64]{0:T(256)(128)(2,1)}, u32[]{:S(2)}) copy-start(bf16[64]{0:T(256)(128)(2,1)} %param.29) | copy-start | bytes 388
  206.2 417.4 %collective-permute-start.3 = (bf16[512,8192]{1,0:T(8,128)(2,1)}, bf16[512,8192]{1,0:T(8,128)(2,1)}, u32[]{:S(2)}, u32[]{:S(2)}) collective-permute-start(bf16[512,8192]{1,0:T(8,128)(2,1)} %maximum_select_fusion.3), channel_id=1, source_target_pairs={{0,8},{1,9},{2,10},{3,11},{4,12},{5,13},{6,14},{7,15},{8,0},{9,1},... | collective-permute-start | bytes 25165832 | tf_op jit(solution)/shard_map/ppermute | solution.py:21
  517.4 53.6 %copy-start.42 = (f32[2048]{0:T(1024)}, f32[2048]{0:T(1024)S(1)}, u32[]{:S(2)}) copy-start(f32[2048]{0:T(1024)S(1)} %convert_element_type.262) | copy-start | bytes 24580
  525.9 45.1 copy-start.49
  555.2 63.3 %all-to-all-start = ((bf16[4,2,65536]{2,1,0:T(2,128)(2,1)}), bf16[4,2,65536]{2,1,0:T(2,128)(2,1)}, u32[]{:S(2)}, u32[]{:S(2)}) async-start(bf16[4,2,65536]{2,1,0:T(2,128)(2,1)} %reshape.873), calls=%async_computation | async-start | bytes 2097152 | tf_op jit(solution)/shard_map/all_to_all | solution.py:139
  571.0 7.2 copy-start.25
  618.5 411.7 %all-to-all-start.2 = ((bf16[4,2,65536]{2,1,0:T(2,128)(2,1)}), bf16[4,2,65536]{2,1,0:T(2,128)(2,1)}, u32[]{:S(2)}, u32[]{:S(2)}) async-start(bf16[4,2,65536]{2,1,0:T(2,128)(2,1)} %reshape.875), calls=%async_computation.2 | async-start | bytes 2097152 | tf_op jit(solution)/shard_map/all_to_all | solution.py:138
  644.1 1226.1 %collective-permute-start.4 = (bf16[1024,8192]{1,0:T(8,128)(2,1)}, bf16[1024,8192]{1,0:T(8,128)(2,1)}, u32[]{:S(2)}, u32[]{:S(2)}) collective-permute-start(bf16[1024,8192]{1,0:T(8,128)(2,1)} %maximum_select_fusion.2), channel_id=1, source_target_pairs={{0,16},{1,17},{2,18},{3,19},{4,20},{5,21},{6,22},{7,23},{8,24},{9,... | collective-permute-start | bytes 50331656 | tf_op jit(solution)/shard_map/ppermute | solution.py:21
  1030.3 707.6 %all-to-all-start.1 = ((bf16[4,2,65536]{2,1,0:T(2,128)(2,1)}), bf16[4,2,65536]{2,1,0:T(2,128)(2,1)}, u32[]{:S(2)}, u32[]{:S(2)}) async-start(bf16[4,2,65536]{2,1,0:T(2,128)(2,1)} %reshape.877), calls=%async_computation.1 | async-start | bytes 2097152 | tf_op jit(solution)/shard_map/all_to_all | solution.py:137
  1043.8 703.3 %copy-start.22 = (bf16[1024,8,64]{0,2,1:T(8,128)(2,1)}, bf16[1024,8,64]{0,2,1:T(8,128)(2,1)S(1)}, u32[]{:S(2)}) copy-start(bf16[1024,8,64]{0,2,1:T(8,128)(2,1)S(1)} %reshape.847) | copy-start | bytes 3145732
  1747.1 18.8 copy-start.16
  1751.8 5.9 copy-start
  1751.8 5.9 copy-start.47
  1751.8 5.9 copy-start.32
  1757.7 8.2 copy-start.30
  1790.4 30.6 all-to-all-start.3
  1798.0 645.8 %reduce-scatter.14.cloned.1.call-start = ((), (), s32[]{:S(2)}) async-start(), calls=%async_computation.25 | async-start | bytes 17301504 | tf_op jit(solution)/shard_map/reduce_scatter | solution.py:313
  1833.5 85.5 %copy-start.13 = (f32[256,2048]{1,0:T(8,128)}, f32[256,2048]{1,0:T(8,128)S(1)}, u32[]{:S(2)}) copy-start(f32[256,2048]{1,0:T(8,128)S(1)} %get-tuple-element.113) | copy-start | bytes 6291460
  1833.8 36.4 copy-start.18
  1919.0 16.7 copy-start.26
  1938.0 8.2 copy-start.11
  1953.6 19.4 copy-start.46
  1953.6 19.4 copy-start.53
  1953.7 19.5 copy-start.48
  1953.7 19.5 copy-start.55
  1966.0 35.3 all-to-all-start.4
  2004.1 20.0 copy-start.20
  2004.1 20.0 slice-start
  2004.1 20.0 slice-start.1
  2012.0 9.7 copy-start.17
  2012.0 12.1 slice-start.2
  2012.0 12.1 slice-start.3
  2033.6 8.0 copy-start.35
  2050.2 28.0 copy-start.23
  2062.0 48.1 all-to-all-start.6
  2078.2 10.6 copy-start.31
  2110.1 41.3 all-to-all-start.5
  2123.3 320.6 %reduce-scatter.8.cloned.1.call-start = ((), (), s32[]{:S(2)}) async-start(), calls=%async_computation.22 | async-start | bytes 17301504 | tf_op jit(solution)/shard_map/reduce_scatter | solution.py:304
  2128.3 36.0 copy-start.7
  2176.7 381.2 %reduce-scatter.10.cloned.1.call-start = ((), (), s32[]{:S(2)}) async-start(), calls=%async_computation.23 | async-start | bytes 17301504 | tf_op jit(solution)/shard_map/reduce_scatter | solution.py:307
  2186.3 558.9 %reduce-scatter.12.cloned.1.call-start = ((), (), s32[]{:S(2)}) async-start(), calls=%async_computation.24 | async-start | bytes 17301504 | tf_op jit(solution)/shard_map/reduce_scatter | solution.py:310
  2269.2 8.3 copy-start.33
  2277.5 1179.3 %reduce-scatter.16.cloned.1.call-start = ((), (), s32[]{:S(2)}) async-start(), calls=%async_computation.26 | async-start | bytes 69206016 | tf_op jit(solution)/shard_map/reduce_scatter | solution.py:213
  2305.1 1865.0 %reduce-scatter.18.cloned.1.call-start = ((), (), s32[]{:S(2)}) async-start(), calls=%async_computation.27 | async-start | bytes 69206016 | tf_op jit(solution)/shard_map/reduce_scatter | solution.py:218
  2331.3 2551.8 %reduce-scatter.20.cloned.1.call-start = ((), (), s32[]{:S(2)}) async-start(), calls=%async_computation.28 | async-start | bytes 69206016 | tf_op jit(solution)/shard_map/reduce_scatter | solution.py:193
  2360.3 17.7 copy-start.8
  2360.3 17.7 copy-start.10
  2360.3 17.7 copy-start.24
  2360.3 17.7 copy-start.39
  2378.1 10.1 slice-start.6
  2380.7 7.4 slice-start.7
  2380.7 11.7 slice-start.4
  2392.5 47.8 copy-start.12
  (29 other events, 88.8 us)
Sparse Core Ops, SparseCore 0:
  10.9 91.0 all-gather.7
  104.8 94.4 all-gather.9
  202.2 107.5 all-gather.11
  312.5 108.8 all-gather.13
  424.1 634.7 all-gather.17
  1061.5 269.5 all-gather.15
  1334.0 269.4 all-gather.19
  1946.3 210.5 reduce-scatter.13
  2176.8 191.8 reduce-scatter.7
  2371.4 186.3 reduce-scatter.9
  2560.7 184.5 reduce-scatter.11
  2748.0 708.7 reduce-scatter.15
  3459.8 710.2 reduce-scatter.17
  4172.8 710.2 reduce-scatter.19
